TPU v7x, 32 devices: a whole 2x2x4 slice. The times are simulated.
32 devices in a mesh: group: 2 (over x), mod: 4 (over y, core), dir: 4 (over z).
Axes of the slice: x: 2, y: 2, z: 4, core: 2. Of those that a mesh axis runs over, the one named last changes fastest.
Arguments:
- screens: float32 [8, 512, 512], P('group', 'mod'), parts along dimension 0, may hold values from -6 to 6
- footprint: int32 [8, 4, 2], P(('group', 'dir')), parts along dimension 0, may hold values from 0 to 191
- fraction: int32 [8, 4, 2], P(('group', 'dir')), parts along dimension 0, may hold values from 0 to 15
- tilt_steps: int32 [16, 2], P(('group', 'mod')), parts along dimension 0, may hold values from -64 to 64
- facet_shift: int32 [4, 2], replicated, may hold values from 80 to 160
Outputs:
- detector: float32 [8, 640, 640], P(('group', 'dir'), 'mod'), parts along dimension 0
There are 2 independent parts, one for each index of `group`. A program takes and returns all parts, laid end to end along the dimension named above; an argument that names none is the same for every part. Nothing has to cross between parts.
All inputs are finite; a program needn't handle non-finite values.
Results may differ from a plain program's by a relative error of at most 0.0055.
Values may be sent and summed in bfloat16 or wider, within the bound.
A program may use at most 64 MiB of HBM per device.

v0:
```python
import functools
import math

import jax
import jax.numpy as jnp
import numpy as np
from jax import lax
from jax.experimental import pallas as pl
from jax.experimental.pallas import tpu as pltpu
from jax.sharding import PartitionSpec as P

P_SIZE = 320
PAD = 640
WIDE = 384
HALF = P_SIZE // 2
MESH = pl.DeviceIdType.MESH
F32 = jnp.float32
BF16 = jnp.bfloat16


def tables(blocks):
    order = np.concatenate([np.arange(0, PAD, 2), np.arange(1, PAD, 2)])

    def parts(first, second, sign):
        turn = np.mod((first - PAD // 2)[:, None] * (second - PAD // 2)[None, :], PAD)
        angle = sign * 2.0 * np.pi / PAD * turn
        return np.cos(angle) / np.sqrt(PAD), np.sin(angle) / np.sqrt(PAD)

    pupil = np.arange(P_SIZE) + (PAD - P_SIZE) // 2
    padded = np.arange(WIDE) + (PAD - P_SIZE) // 2
    d_re, d_im = parts(order, pupil, -1.0)
    left_pupil = np.stack([np.concatenate([d_re, -d_im], 1), np.concatenate([d_im, d_re], 1)])
    keep = (np.arange(WIDE) < P_SIZE)[:, None]
    right_pupil = np.stack([part * keep for part in parts(padded, order, -1.0)])
    upper = np.arange(PAD // 2)
    g_re, g_im = parts(upper, order, 1.0)
    pieces = []
    for parity in range(2):
        cut = slice(parity * P_SIZE, (parity + 1) * P_SIZE)
        pieces.append(np.concatenate([g_re[:, cut], -g_im[:, cut]], 1))
        pieces.append(np.concatenate([g_im[:, cut], g_re[:, cut]], 1))
    left_focal = np.stack(pieces).reshape(4, blocks // 2, PAD // blocks, PAD)
    right_focal = np.stack(parts(order, np.arange(PAD), 1.0))
    return [np.asarray(t, dtype=BF16) for t in (left_pupil, right_pupil, left_focal, right_focal)]


def turn_parts(steps, period):
    quarter = jnp.round(steps * (4.0 / period))
    rest = (steps - quarter * (period / 4.0)) * (2.0 * math.pi / period)
    return quadrant_parts(rest, quarter)


def radian_parts(angle):
    quarter = jnp.round(angle * (2.0 / math.pi))
    coarse = 1.5703125
    fine = math.pi / 2 - coarse
    rest = (angle - quarter * coarse) - quarter * fine
    return quadrant_parts(rest, quarter)


def quadrant_parts(rest, quarter):
    sq = rest * rest
    sine = rest * (1.0 + sq * (-1.0 / 6 + sq * (1.0 / 120 + sq * (-1.0 / 5040 + sq * (1.0 / 362880)))))
    cosine = 1.0 + sq * (-0.5 + sq * (1.0 / 24 + sq * (-1.0 / 720 + sq * (1.0 / 40320))))
    index = quarter.astype(jnp.int32)
    odd = (index & 1) == 1
    cos_out = jnp.where(odd, sine, cosine)
    sin_out = jnp.where(odd, cosine, sine)
    cos_out = jnp.where(((index + 1) & 2) == 2, -cos_out, cos_out)
    sin_out = jnp.where((index & 2) == 2, -sin_out, sin_out)
    return cos_out, sin_out


def iota(shape, axis):
    return lax.broadcasted_iota(jnp.int32, shape, axis)


def dot(left, right):
    return jnp.dot(left, right, preferred_element_type=F32)


def kernel(
    n, layers, band, points,
    footprint, fraction, tilt, facet,
    screens, left_pupil_hbm, right_pupil_hbm, left_focal_hbm, right_focal_hbm,
    out,
    lp, rp_in, rp, lf, rf_in, rf,
    snd1, rcv1, snd2, rcv2, fsnd, frcv,
    modb, mbuf, mk, bk, mask_c, mask_s, acc, isnd, ircv, ysnd, yrcv,
    load_sem, s1, r1, s2, r2, s3, r3, s4, r4, s5, r5,
):
    m = n // 2
    rows = PAD // n
    me = lax.axis_index("mod")
    core = lax.rem(me, 2)
    chip = me // 2
    other = 1 - core
    partner = chip * 2 + other

    loads = [
        pltpu.make_async_copy(src, dst, load_sem.at[i])
        for i, (src, dst) in enumerate(
            ((right_pupil_hbm, rp_in), (left_pupil_hbm, lp), (left_focal_hbm, lf), (right_focal_hbm, rf_in))
        )
    ]
    for load in loads:
        load.start()

    barrier = pltpu.get_barrier_semaphore()
    for k in range(1, n):
        pl.semaphore_signal(
            barrier, inc=1, device_id={"mod": lax.rem(me + k, n)}, device_id_type=MESH
        )

    def send(src, dst, send_sem, recv_sem, target):
        return pltpu.make_async_remote_copy(
            src_ref=src, dst_ref=dst, send_sem=send_sem, recv_sem=recv_sem,
            device_id={"mod": target}, device_id_type=MESH,
        )

    split = []
    for layer in range(layers):
        frac = fraction[0, layer, 1].astype(F32) / 16.0
        gap = iota((screens.shape[2], WIDE), 0) - iota((screens.shape[2], WIDE), 1) - footprint[0, layer, 1]
        pick = jnp.where(gap == 0, 1.0 - frac, jnp.where(gap == 1, frac, 0.0)).astype(BF16)
        whole = screens[layer]
        high = whole.astype(BF16)
        low = (whole - high.astype(F32)).astype(BF16)
        value = dot(high, pick) + dot(low, pick)
        value_high = value.astype(BF16)
        split.append((value_high, (value - value_high.astype(F32)).astype(BF16)))

    def partial(first):
        total = jnp.zeros((HALF, WIDE), F32)
        for layer in range(layers):
            frac = fraction[0, layer, 0].astype(F32) / 16.0
            gap = (
                iota((HALF, band), 1) + me * band
                - iota((HALF, band), 0) - first - footprint[0, layer, 0]
            )
            pick = jnp.where(gap == 0, 1.0 - frac, jnp.where(gap == 1, frac, 0.0)).astype(BF16)
            total = total + dot(pick, split[layer][0]) + dot(pick, split[layer][1])
        return total

    snd1[...] = partial(other * HALF)
    pl.semaphore_wait(barrier, n - 1)
    first_copy = send(snd1, rcv1, s1, r1, partner)
    first_copy.start()

    snd2[...] = partial(core * HALF)

    def mask_chunk(chunk):
        parity, lower = chunk // 2, chunk % 2
        along_u = 2 * (iota((HALF, 1), 0) + lower * HALF) + parity - PAD // 2
        lane = iota((1, PAD), 1)
        spot = jnp.where(lane < P_SIZE, lane, lane - P_SIZE)
        along_v = jnp.where(lane < P_SIZE, 2 * spot, 2 * spot + 1) - PAD // 2
        right = along_v >= 0
        sign = 2 * lower - 1
        row_shift = sign * jnp.where(right, facet[2 * lower + 1, 0], facet[2 * lower, 0])
        col_shift = jnp.where(right, facet[2 * lower + 1, 1], -facet[2 * lower, 1])
        steps = (
            row_shift.astype(F32) * along_u.astype(F32)
            + (col_shift * along_v).astype(F32)
        )
        cos_part, sin_part = turn_parts(-steps, float(PAD))
        mask_c[chunk] = cos_part
        mask_s[chunk] = sin_part

    mask_chunk(0)
    first_copy.wait()
    snd2[...] = snd2[...] + rcv1[...]
    second = []
    for k in range(1, m):
        copy = send(
            snd2, rcv2.at[k - 1], s2.at[k - 1], r2.at[k - 1], lax.rem(me + 2 * k, n)
        )
        copy.start()
        second.append(copy)

    mask_chunk(1)
    mask_chunk(2)
    mask_chunk(3)
    for load in loads:
        load.wait()
    rp[0:WIDE, 0:PAD] = rp_in[0]
    rp[0:WIDE, PAD:] = rp_in[1]
    rp[WIDE:, 0:PAD] = -rp_in[1]
    rp[WIDE:, PAD:] = rp_in[0]
    rf[0:PAD, 0:PAD] = rf_in[0]
    rf[0:PAD, PAD:] = rf_in[1]
    rf[PAD:, 0:PAD] = -rf_in[1]
    rf[PAD:, PAD:] = rf_in[0]

    for copy in second:
        copy.wait()
    phase = snd2[...]
    for k in range(1, m):
        phase = phase + rcv2[k - 1]
    along_y = 2 * (iota((HALF, 1), 0) + core * HALF) - P_SIZE + 1
    along_x = 2 * iota((1, WIDE), 1) - P_SIZE + 1
    radius = along_y * along_y + along_x * along_x
    edge = P_SIZE * 28 // 100 * (P_SIZE * 28 // 100)
    inside = (radius <= P_SIZE * P_SIZE) & (radius >= edge)
    cos_part, sin_part = radian_parts(phase)
    fsnd[0] = jnp.where(inside, cos_part, 0.0).astype(BF16)
    fsnd[1] = jnp.where(inside, sin_part, 0.0).astype(BF16)
    third = send(fsnd, frcv, s3, r3, partner)
    third.start()

    def pupil_stage(field, which):
        wide_re = field[0].astype(F32)
        wide_im = field[1].astype(F32)
        for p in range(points):
            row_steps = tilt[p, 0].astype(F32) * (iota((HALF, 1), 0) + which * HALF).astype(F32)
            col_steps = tilt[p, 1].astype(F32) * iota((1, WIDE), 1).astype(F32)
            row_c, row_s = turn_parts(row_steps, 8.0 * PAD)
            col_c, col_s = turn_parts(col_steps, 8.0 * PAD)
            tilt_c = row_c * col_c - row_s * col_s
            tilt_s = row_s * col_c + row_c * col_s
            modb[p * HALF : (p + 1) * HALF, 0:WIDE] = (wide_re * tilt_c - wide_im * tilt_s).astype(BF16)
            modb[p * HALF : (p + 1) * HALF, WIDE:] = (wide_re * tilt_s + wide_im * tilt_c).astype(BF16)
        start = pl.multiple_of(which * HALF, 32)
        for p in range(points):
            wide = dot(modb[p * HALF : (p + 1) * HALF, :], rp[...])
            mbuf[pl.ds(start, HALF), p * PAD : (p + 1) * PAD] = wide[:, :PAD].astype(BF16)
            mbuf[pl.ds(start + P_SIZE, HALF), p * PAD : (p + 1) * PAD] = wide[:, PAD:].astype(BF16)

    pupil_stage(fsnd, core)
    third.wait()
    pupil_stage(frcv, other)

    for chunk in range(4):
        parity, lower = chunk // 2, chunk % 2
        cut = slice(chunk * HALF, (chunk + 1) * HALF)
        for p in range(points):
            lanes = slice(p * PAD, (p + 1) * PAD)
            focal_re = dot(lp[0, cut, :], mbuf[:, lanes])
            focal_im = dot(lp[1, cut, :], mbuf[:, lanes])
            mc, ms = mask_c[chunk], mask_s[chunk]
            mk[parity, lower * HALF : (lower + 1) * HALF, lanes] = (
                focal_re * mc - focal_im * ms
            ).astype(BF16)
            mk[parity, P_SIZE + lower * HALF : P_SIZE + (lower + 1) * HALF, lanes] = (
                focal_re * ms + focal_im * mc
            ).astype(BF16)

    for j in range(m):
        for p in range(points):
            lanes = slice(p * PAD, (p + 1) * PAD)
            for part in range(2):
                even = dot(lf[part, j], mk[0, :, lanes])
                odd = dot(lf[2 + part, j], mk[1, :, lanes])
                spot = slice(part * PAD, (part + 1) * PAD)
                bk[p, j, :, spot] = (even + odd).astype(BF16)
                bk[p, j + m, :, spot] = (even - odd).astype(BF16)

    def intensity(block):
        total = None
        for p in range(points):
            image = dot(bk[p, block], rf[...])
            re, im = image[:, :PAD], image[:, PAD:]
            term = re * re + im * im
            total = term if total is None else total + term
        return total

    pending = []
    for k in list(range(1, m)) + [0]:
        target = lax.rem(chip + k, m)
        isnd[k] = intensity(2 * target + other).astype(BF16)
        inner = send(isnd.at[k], ircv.at[k], s4.at[k], r4.at[k], partner)
        inner.start()
        acc[...] = intensity(2 * target + core)
        inner.wait()
        if k > 0:
            ysnd[k - 1] = (acc[...] + ircv[k].astype(F32)).astype(BF16)
            outer = send(
                ysnd.at[k - 1], yrcv.at[k - 1], s5.at[k - 1], r5.at[k - 1], lax.rem(me + 2 * k, n)
            )
            outer.start()
            pending.append(outer)
    total = acc[...] + ircv[0].astype(F32)
    for k, outer in enumerate(pending):
        outer.wait()
        total = total + yrcv[k].astype(F32)
    out[0] = total * (4.0 / (points * n))


def solution(mesh):
    n = mesh.shape["mod"]
    m = n // 2
    rows = PAD // n
    consts = tables(n)

    def shards(screens, footprint, fraction, tilt_steps, facet_shift):
        layers, band, width = screens.shape
        points = tilt_steps.shape[0]
        smem = pl.BlockSpec(memory_space=pltpu.SMEM)
        vmem = pl.BlockSpec(memory_space=pltpu.VMEM)
        anywhere = pl.BlockSpec(memory_space=pl.ANY)
        dma = pltpu.SemaphoreType.DMA
        return pl.pallas_call(
            functools.partial(kernel, n, layers, band, points),
            out_shape=jax.ShapeDtypeStruct((1, rows, PAD), F32),
            in_specs=[smem] * 4 + [vmem] + [anywhere] * 4,
            out_specs=vmem,
            scratch_shapes=[
                pltpu.VMEM((2, PAD, PAD), BF16),
                pltpu.VMEM((2, WIDE, PAD), BF16),
                pltpu.VMEM((2 * WIDE, 2 * PAD), BF16),
                pltpu.VMEM((4, m, rows, PAD), BF16),
                pltpu.VMEM((2, PAD, PAD), BF16),
                pltpu.VMEM((2 * PAD, 2 * PAD), BF16),
                pltpu.VMEM((HALF, WIDE), F32),
                pltpu.VMEM((HALF, WIDE), F32),
                pltpu.VMEM((HALF, WIDE), F32),
                pltpu.VMEM((m - 1, HALF, WIDE), F32),
                pltpu.VMEM((2, HALF, WIDE), BF16),
                pltpu.VMEM((2, HALF, WIDE), BF16),
                pltpu.VMEM((points * HALF, 2 * WIDE), BF16),
                pltpu.VMEM((PAD, points * PAD), BF16),
                pltpu.VMEM((2, PAD, points * PAD), BF16),
                pltpu.VMEM((points, n, rows, 2 * PAD), BF16),
                pltpu.VMEM((4, HALF, PAD), F32),
                pltpu.VMEM((4, HALF, PAD), F32),
                pltpu.VMEM((rows, PAD), F32),
                pltpu.VMEM((m, rows, PAD), BF16),
                pltpu.VMEM((m, rows, PAD), BF16),
                pltpu.VMEM((m - 1, rows, PAD), BF16),
                pltpu.VMEM((m - 1, rows, PAD), BF16),
                dma((4,)),
                dma, dma,
                dma((m - 1,)), dma((m - 1,)),
                dma, dma,
                dma((m,)), dma((m,)),
                dma((m - 1,)), dma((m - 1,)),
            ],
            compiler_params=pltpu.CompilerParams(
                collective_id=0, has_side_effects=True, vmem_limit_bytes=60 * 1024 * 1024
            ),
        )(footprint, fraction, tilt_steps, facet_shift, screens, *[jnp.asarray(t) for t in consts])

    placed = (
        P("group", "mod", None),
        P(("group", "dir"), None, None),
        P(("group", "dir"), None, None),
        P(("group", "mod"), None),
        P(),
    )
    return jax.shard_map(
        shards,
        mesh=mesh,
        in_specs=placed,
        out_specs=P(("group", "dir"), "mod", None),
        check_vma=False,
    )
```

profile of v0, /device:TPU:0, one launch (start us, length us, event | category | flops | bytes accessed | tf_op | source)
XLA Modules:
  0.0 38.1 jit_solution(4526958191222386723)
XLA Ops:
  0.0 1.3 %copy.10.footprint = s32[1,4,2]{2,1,0:T(4,128)} copy(s32[1,4,2]{1,2,0:T(2,128)} %param.10) | data formatting | bytes 64 | tf_op args[1]
  1.3 1.3 %copy.11.fraction = s32[1,4,2]{2,1,0:T(4,128)} copy(s32[1,4,2]{1,2,0:T(2,128)} %param.11) | data formatting | bytes 64 | tf_op args[2]
  2.7 1.3 %copy.12.facet = s32[4,2]{1,0:T(4,128)} copy(s32[4,2]{0,1:T(2,128)} %param.13) | data formatting | bytes 64 | tf_op args[4]
  4.0 32.3 %shard_map.91 = f32[1,160,640]{2,1,0:T(8,128)} custom-call(s32[1,4,2]{2,1,0:T(4,128)} %copy.10.footprint, s32[1,4,2]{2,1,0:T(4,128)} %copy.11.fraction, s32[2,2]{1,0:T(2,128)} %tilt.1, s32[4,2]{1,0:T(4,128)} %copy.12.facet, f32[4,128,512]{2,1,0:T(8,128)} %screens.1, bf16[2,640,640]{2,1,0:T(8,128)(2,1)} %constant.8.clone.left_pupil_hbm, ...), custom_call_target="tpu_custom_call" | custom-call | tf_op jit(solution)/shard_map/pallas_call | solution.py:302
  36.3 1.8 %copy.14 = f32[1,160,640]{2,1,0:T(8,128)} copy(f32[1,160,640]{2,1,0:T(8,128)} %shard_map.91) | data formatting | bytes 819200
where the time goes:
time: 38.3 us; the launch traced here: 38.1 us
  Pallas kernels  32.3 us (84%)
  local copies, waits for them, and re-layouts  5.78 us (15%)
    pallas_call x1, Pallas kernels, shards(): pl.pallas_call(functools.partial(kernel, n, layers, band, points), out_sh...  32.3 us
    unnamed x4, local copies, waits for them, and re-layouts  5.78 us

commit v1 on v0

v1 whole, which is shorter than its diff:
```python
import functools
import math

import jax
import jax.numpy as jnp
import numpy as np
from jax import lax
from jax.experimental import pallas as pl
from jax.experimental.pallas import tpu as pltpu
from jax.sharding import PartitionSpec as P

P_SIZE = 320
PAD = 640
WIDE = 384
HALF = P_SIZE // 2
MESH = pl.DeviceIdType.MESH
F32 = jnp.float32
BF16 = jnp.bfloat16


def tables(chips, pieces, rows):
    order = np.concatenate([np.arange(0, PAD, 2), np.arange(1, PAD, 2)])

    def parts(first, second, sign):
        turn = np.mod((first - PAD // 2)[:, None] * (second - PAD // 2)[None, :], PAD)
        angle = sign * 2.0 * np.pi / PAD * turn
        return np.cos(angle) / np.sqrt(PAD), np.sin(angle) / np.sqrt(PAD)

    pupil = np.arange(P_SIZE) + (PAD - P_SIZE) // 2
    padded = np.arange(WIDE) + (PAD - P_SIZE) // 2
    d_re, d_im = parts(order, pupil, -1.0)
    left_pupil = np.stack([np.concatenate([d_re, -d_im], 1), np.concatenate([d_im, d_re], 1)])
    keep = (np.arange(WIDE) < P_SIZE)[:, None]
    right_pupil = np.stack([part * keep for part in parts(padded, order, -1.0)])
    upper = np.arange(PAD // 2)
    g_re, g_im = parts(upper, order, 1.0)
    left_focal = []
    for parity in range(2):
        cut = slice(parity * P_SIZE, (parity + 1) * P_SIZE)
        left_focal.append(
            [
                np.concatenate([g_re[:, cut], -g_im[:, cut]], 1),
                np.concatenate([g_im[:, cut], g_re[:, cut]], 1),
            ]
        )
    left_focal = np.asarray(left_focal).reshape(2, 2, chips, pieces, rows, PAD)
    left_focal = left_focal.transpose(0, 3, 1, 2, 4, 5).reshape(2, pieces, P_SIZE * 2 // pieces, PAD)
    right_focal = np.stack(parts(order, np.arange(PAD), 1.0))
    return [np.asarray(t, dtype=BF16) for t in (left_pupil, right_pupil, left_focal, right_focal)]


def turn_parts(steps, period):
    quarter = jnp.round(steps * (4.0 / period))
    rest = (steps - quarter * (period / 4.0)) * (2.0 * math.pi / period)
    return quadrant_parts(rest, quarter.astype(jnp.int32))


def code_parts(code):
    quarter = (code + 8192) >> 14
    rest = (code - (quarter << 14)).astype(F32) * (2.0 * math.pi / 65536)
    return quadrant_parts(rest, quarter)


def wrapped(code):
    return ((code << 16) >> 16).astype(jnp.int16)


def quadrant_parts(rest, index):
    sq = rest * rest
    sine = rest * (1.0 + sq * (-1.0 / 6 + sq * (1.0 / 120 + sq * (-1.0 / 5040 + sq * (1.0 / 362880)))))
    cosine = 1.0 + sq * (-0.5 + sq * (1.0 / 24 + sq * (-1.0 / 720 + sq * (1.0 / 40320))))
    odd = (index & 1) == 1
    cos_out = jnp.where(odd, sine, cosine)
    sin_out = jnp.where(odd, cosine, sine)
    cos_out = jnp.where(((index + 1) & 2) == 2, -cos_out, cos_out)
    sin_out = jnp.where((index & 2) == 2, -sin_out, sin_out)
    return cos_out, sin_out


def iota(shape, axis):
    return lax.broadcasted_iota(jnp.int32, shape, axis)


def dot(left, right):
    return jnp.dot(left, right, preferred_element_type=F32)


def kernel(
    n, pieces, layers, band, points,
    footprint, fraction, tilt, facet,
    screens, left_pupil_hbm, right_pupil_hbm, left_focal_hbm, right_focal_hbm,
    out,
    lp, rp_in, rp, lf, rf_in, rf,
    own, snd1, rcv1, snd2, rcv2, fsnd, frcv,
    modb, mbuf, mk, bk, mask_c, mask_s, both, acc, isnd, ircv, ysnd, yrcv,
    load_sem, s1, r1, s2, r2, s3, r3, s4, r4, s5, r5,
):
    m = n // 2
    rows = PAD // n // pieces
    part_rows = HALF // 2
    me = lax.axis_index("mod")
    core = lax.rem(me, 2)
    chip = me // 2
    other = 1 - core
    partner = chip * 2 + other

    loads = [
        pltpu.make_async_copy(src, dst, load_sem.at[i])
        for i, (src, dst) in enumerate(
            ((right_pupil_hbm, rp_in), (left_pupil_hbm, lp), (left_focal_hbm, lf), (right_focal_hbm, rf_in))
        )
    ]
    for load in loads:
        load.start()

    barrier = pltpu.get_barrier_semaphore()
    for k in range(1, n):
        pl.semaphore_signal(
            barrier, inc=1, device_id={"mod": lax.rem(me + k, n)}, device_id_type=MESH
        )

    def send(src, dst, send_sem, recv_sem, target):
        return pltpu.make_async_remote_copy(
            src_ref=src, dst_ref=dst, send_sem=send_sem, recv_sem=recv_sem,
            device_id={"mod": target}, device_id_type=MESH,
        )

    split = []
    for layer in range(layers):
        frac = fraction[0, 1, layer].astype(F32) / 16.0
        gap = iota((screens.shape[2], WIDE), 0) - iota((screens.shape[2], WIDE), 1) - footprint[0, 1, layer]
        pick = jnp.where(gap == 0, 1.0 - frac, jnp.where(gap == 1, frac, 0.0)).astype(BF16)
        whole = screens[layer]
        high = whole.astype(BF16)
        low = (whole - high.astype(F32)).astype(BF16)
        value = dot(high, pick) + dot(low, pick)
        value_high = value.astype(BF16)
        split.append((value_high, (value - value_high.astype(F32)).astype(BF16)))

    def partial(first):
        total = jnp.zeros((part_rows, WIDE), F32)
        for layer in range(layers):
            frac = fraction[0, 0, layer].astype(F32) / 16.0
            gap = (
                iota((part_rows, band), 1) + me * band
                - iota((part_rows, band), 0) - first - footprint[0, 0, layer]
            )
            pick = jnp.where(gap == 0, 1.0 - frac, jnp.where(gap == 1, frac, 0.0)).astype(BF16)
            total = total + dot(pick, split[layer][0]) + dot(pick, split[layer][1])
        return jnp.round(total * (32768.0 / math.pi)).astype(jnp.int32)

    first = []
    for q in range(2):
        snd1[q] = wrapped(partial(other * HALF + q * part_rows))
        if q == 0:
            pl.semaphore_wait(barrier, n - 1)
        copy = send(snd1.at[q], rcv1.at[q], s1.at[q], r1.at[q], partner)
        copy.start()
        first.append(copy)
    for q in range(2):
        own[q] = partial(core * HALF + q * part_rows)

    def mask_chunk(chunk):
        parity, lower = chunk // 2, chunk % 2
        along_u = 2 * (iota((HALF, 1), 0) + lower * HALF) + parity - PAD // 2
        lane = iota((1, PAD), 1)
        spot = jnp.where(lane < P_SIZE, lane, lane - P_SIZE)
        along_v = jnp.where(lane < P_SIZE, 2 * spot, 2 * spot + 1) - PAD // 2
        right = along_v >= 0
        sign = 2 * lower - 1
        cut = slice(lower * HALF, (lower + 1) * HALF)
        row_shift = sign * jnp.where(right, facet[0, 2 * lower + 1], facet[0, 2 * lower])
        col_shift = jnp.where(right, facet[1, 2 * lower + 1], -facet[1, 2 * lower])
        steps = (
            row_shift.astype(F32) * along_u.astype(F32)
            + (col_shift * along_v).astype(F32)
        )
        cos_part, sin_part = turn_parts(-steps, float(PAD))
        mask_c[parity, cut] = cos_part
        mask_s[parity, cut] = sin_part

    mask_chunk(0)
    second = []
    for q in range(2):
        first[q].wait()
        total = own[q] + rcv1[q].astype(jnp.int32)
        own[q] = total
        snd2[q] = wrapped(total)
        copies = []
        for k in range(1, m):
            copy = send(
                snd2.at[q], rcv2.at[k - 1, q], s2.at[k - 1, q], r2.at[k - 1, q], lax.rem(me + 2 * k, n)
            )
            copy.start()
            copies.append(copy)
        second.append(copies)

    mask_chunk(1)
    mask_chunk(2)
    mask_chunk(3)
    for load in loads:
        load.wait()
    rp[0:WIDE, 0:PAD] = rp_in[0]
    rp[0:WIDE, PAD:] = rp_in[1]
    rp[WIDE:, 0:PAD] = -rp_in[1]
    rp[WIDE:, PAD:] = rp_in[0]
    rf[0:PAD, 0:PAD] = rf_in[0]
    rf[0:PAD, PAD:] = rf_in[1]
    rf[PAD:, 0:PAD] = -rf_in[1]
    rf[PAD:, PAD:] = rf_in[0]

    third = []
    for q in range(2):
        code = own[q]
        for k in range(1, m):
            second[q][k - 1].wait()
            code = code + rcv2[k - 1, q].astype(jnp.int32)
        along_y = 2 * (iota((part_rows, 1), 0) + core * HALF + q * part_rows) - P_SIZE + 1
        along_x = 2 * iota((1, WIDE), 1) - P_SIZE + 1
        radius = along_y * along_y + along_x * along_x
        edge = P_SIZE * 28 // 100 * (P_SIZE * 28 // 100)
        inside = (radius <= P_SIZE * P_SIZE) & (radius >= edge)
        cos_part, sin_part = code_parts(code)
        fsnd[q, 0] = jnp.where(inside, cos_part, 0.0).astype(BF16)
        fsnd[q, 1] = jnp.where(inside, sin_part, 0.0).astype(BF16)
        copy = send(fsnd.at[q], frcv.at[q], s3.at[q], r3.at[q], partner)
        copy.start()
        third.append(copy)

    def pupil_stage(field, which):
        for q in range(2):
            wide_re = field[q, 0].astype(F32)
            wide_im = field[q, 1].astype(F32)
            for p in range(points):
                row_ids = iota((part_rows, 1), 0) + which * HALF + q * part_rows
                row_steps = tilt[p, 0].astype(F32) * row_ids.astype(F32)
                col_steps = tilt[p, 1].astype(F32) * iota((1, WIDE), 1).astype(F32)
                row_c, row_s = turn_parts(row_steps, 8.0 * PAD)
                col_c, col_s = turn_parts(col_steps, 8.0 * PAD)
                tilt_c = row_c * col_c - row_s * col_s
                tilt_s = row_s * col_c + row_c * col_s
                cut = slice(p * HALF + q * part_rows, p * HALF + (q + 1) * part_rows)
                modb[cut, 0:WIDE] = (wide_re * tilt_c - wide_im * tilt_s).astype(BF16)
                modb[cut, WIDE:] = (wide_re * tilt_s + wide_im * tilt_c).astype(BF16)
        start = pl.multiple_of(which * HALF, 32)
        wide = dot(modb[...], rp[...]).astype(BF16)
        for p in range(points):
            cut = slice(p * HALF, (p + 1) * HALF)
            mbuf[pl.ds(start, HALF), p * PAD : (p + 1) * PAD] = wide[cut, :PAD]
            mbuf[pl.ds(start + P_SIZE, HALF), p * PAD : (p + 1) * PAD] = wide[cut, PAD:]

    pupil_stage(fsnd, core)
    for copy in third:
        copy.wait()
    pupil_stage(frcv, other)

    for parity in range(2):
        cut = slice(parity * P_SIZE, (parity + 1) * P_SIZE)
        for p in range(points):
            lanes = slice(p * PAD, (p + 1) * PAD)
            focal_re = dot(lp[0, cut, :], mbuf[:, lanes])
            focal_im = dot(lp[1, cut, :], mbuf[:, lanes])
            mc = mask_c[parity]
            ms = mask_s[parity]
            mk[parity, :P_SIZE, lanes] = (focal_re * mc - focal_im * ms).astype(BF16)
            mk[parity, P_SIZE:, lanes] = (focal_re * ms + focal_im * mc).astype(BF16)

    def focal_stage(piece):
        even = dot(lf[0, piece], mk[0])
        odd = dot(lf[1, piece], mk[1])
        for sign in range(2):
            value = ((even + odd) if sign == 0 else (even - odd)).astype(BF16)
            for part in range(2):
                for j in range(m):
                    block = j + sign * m
                    base = (part * m + j) * rows
                    for p in range(points):
                        spot = ((block % 2) * points + p) * rows
                        bk[block // 2, piece, spot : spot + rows, part * PAD : (part + 1) * PAD] = value[
                            base : base + rows, p * PAD : (p + 1) * PAD
                        ]

    waiting = []

    def drain():
        while waiting:
            k, piece, inner = waiting.pop()
            inner.wait()
            ysnd[k - 1, piece] = (acc[k, piece] + ircv[k, piece].astype(F32)).astype(BF16)
            outer = send(
                ysnd.at[k - 1, piece], yrcv.at[k - 1, piece], s5.at[k - 1, piece], r5.at[k - 1, piece],
                lax.rem(me + 2 * k, n),
            )
            outer.start()
            pending.append(outer)

    def image_stage(k, piece):
        target = lax.rem(chip + k, m)
        image = dot(bk[target, piece], rf[...])
        power = image[:, :PAD] * image[:, :PAD] + image[:, PAD:] * image[:, PAD:]
        for half in range(2):
            total = None
            for p in range(points):
                spot = (half * points + p) * rows
                term = power[spot : spot + rows]
                total = term if total is None else total + term
            both[half] = total
        isnd[k, piece] = both[other].astype(BF16)
        acc[k, piece] = both[core]
        inner = send(isnd.at[k, piece], ircv.at[k, piece], s4.at[k, piece], r4.at[k, piece], partner)
        inner.start()
        return inner

    pending = []
    for piece in range(pieces):
        focal_stage(piece)
        drain()
        for k in range(1, m):
            inner = image_stage(k, piece)
            drain()
            waiting.append((k, piece, inner))
    last = []
    for piece in range(pieces):
        last.append(image_stage(0, piece))
        drain()
    for outer in pending:
        outer.wait()
    for piece in range(pieces):
        last[piece].wait()
        total = acc[0, piece] + ircv[0, piece].astype(F32)
        for k in range(1, m):
            total = total + yrcv[k - 1, piece].astype(F32)
        out[0, piece * rows : (piece + 1) * rows] = total * (4.0 / (points * n))


def solution(mesh):
    n = mesh.shape["mod"]
    m = n // 2
    whole_rows = PAD // n
    pieces = 2 if whole_rows % 32 == 0 else 1
    rows = whole_rows // pieces
    consts = tables(m, pieces, rows)
    part_rows = HALF // 2

    def shards(screens, footprint, fraction, tilt_steps, facet_shift):
        layers, band, width = screens.shape
        points = tilt_steps.shape[0]
        smem = pl.BlockSpec(memory_space=pltpu.SMEM)
        vmem = pl.BlockSpec(memory_space=pltpu.VMEM)
        anywhere = pl.BlockSpec(memory_space=pl.ANY)
        dma = pltpu.SemaphoreType.DMA
        return pl.pallas_call(
            functools.partial(kernel, n, pieces, layers, band, points),
            out_shape=jax.ShapeDtypeStruct((1, whole_rows, PAD), F32),
            in_specs=[smem] * 4 + [vmem] + [anywhere] * 4,
            out_specs=vmem,
            scratch_shapes=[
                pltpu.VMEM((2, PAD, PAD), BF16),
                pltpu.VMEM((2, WIDE, PAD), BF16),
                pltpu.VMEM((2 * WIDE, 2 * PAD), BF16),
                pltpu.VMEM((2, pieces, 2 * P_SIZE // pieces, PAD), BF16),
                pltpu.VMEM((2, PAD, PAD), BF16),
                pltpu.VMEM((2 * PAD, 2 * PAD), BF16),
                pltpu.VMEM((2, part_rows, WIDE), jnp.int32),
                pltpu.VMEM((2, part_rows, WIDE), jnp.int16),
                pltpu.VMEM((2, part_rows, WIDE), jnp.int16),
                pltpu.VMEM((2, part_rows, WIDE), jnp.int16),
                pltpu.VMEM((m - 1, 2, part_rows, WIDE), jnp.int16),
                pltpu.VMEM((2, 2, part_rows, WIDE), BF16),
                pltpu.VMEM((2, 2, part_rows, WIDE), BF16),
                pltpu.VMEM((points * HALF, 2 * WIDE), BF16),
                pltpu.VMEM((PAD, points * PAD), BF16),
                pltpu.VMEM((2, PAD, points * PAD), BF16),
                pltpu.VMEM((m, pieces, 2 * points * rows, 2 * PAD), BF16),
                pltpu.VMEM((2, P_SIZE, PAD), F32),
                pltpu.VMEM((2, P_SIZE, PAD), F32),
                pltpu.VMEM((2, rows, PAD), F32),
                pltpu.VMEM((m, pieces, rows, PAD), F32),
                pltpu.VMEM((m, pieces, rows, PAD), BF16),
                pltpu.VMEM((m, pieces, rows, PAD), BF16),
                pltpu.VMEM((m - 1, pieces, rows, PAD), BF16),
                pltpu.VMEM((m - 1, pieces, rows, PAD), BF16),
                dma((4,)),
                dma((2,)), dma((2,)),
                dma((m - 1, 2)), dma((m - 1, 2)),
                dma((2,)), dma((2,)),
                dma((m, pieces)), dma((m, pieces)),
                dma((m - 1, pieces)), dma((m - 1, pieces)),
            ],
            compiler_params=pltpu.CompilerParams(
                collective_id=0, has_side_effects=True, vmem_limit_bytes=60 * 1024 * 1024
            ),
        )(footprint.swapaxes(1, 2), fraction.swapaxes(1, 2), tilt_steps, facet_shift.T, screens, *[jnp.asarray(t) for t in consts])

    placed = (
        P("group", "mod", None),
        P(("group", "dir"), None, None),
        P(("group", "dir"), None, None),
        P(("group", "mod"), None),
        P(),
    )
    return jax.shard_map(
        shards,
        mesh=mesh,
        in_specs=placed,
        out_specs=P(("group", "dir"), "mod", None),
        check_vma=False,
    )
```

time: 38.3 us -> 31.3 us (0.82)
  local copies, waits for them, and re-layouts: 5.78 us -> 1.78 us
  Pallas kernels: 32.3 us -> 29.3 us
    unnamed x4 -> x1, local copies, waits for them, and re-layouts: 5.78 us -> 1.78 us
    pallas_call x1, Pallas kernels: 32.3 us -> 29.3 us  [shards(): pl.pallas_call(functools.partial(kernel, n, pieces, layers, band, points)...]
where the time goes in v1:
time: 31.3 us; the launch traced here: 31.1 us
  Pallas kernels  29.3 us (94%)
  local copies, waits for them, and re-layouts  1.78 us (6%)
    pallas_call x1, Pallas kernels, shards(): pl.pallas_call(functools.partial(kernel, n, pieces, layers, band, points)...  29.3 us
    unnamed x1, local copies, waits for them, and re-layouts  1.78 us

profile of v1, /device:TPU:0, one launch (start us, length us, event | category | flops | bytes accessed | tf_op | source)
XLA Modules:
  0.0 31.1 jit_solution(3941223815735901980)
XLA Ops:
  0.0 29.3 %shard_map.91 = f32[1,160,640]{2,1,0:T(8,128)} custom-call(s32[1,2,4]{2,1,0:T(2,128)} %bitcast.3, s32[1,2,4]{2,1,0:T(2,128)} %bitcast.4, s32[2,2]{1,0:T(2,128)} %tilt.1, s32[2,4]{1,0:T(2,128)} %bitcast.5, f32[4,128,512]{2,1,0:T(8,128)} %screens.1, bf16[2,640,640]{2,1,0:T(8,128)(2,1)} %constant.8.clone.left_pupil_hbm, ...), custom_call_target="tpu_custom_call" | custom-call | tf_op jit(solution)/shard_map/pallas_call | solution.py:352
  29.4 1.8 %copy.11 = f32[1,160,640]{2,1,0:T(8,128)} copy(f32[1,160,640]{2,1,0:T(8,128)} %shard_map.91) | data formatting | bytes 819200

commit v2 on v1

--- a/solution.py
+++ b/solution.py
@@ -18,7 +18,7 @@
 BF16 = jnp.bfloat16
 
 
-def tables(chips, pieces, rows):
+def tables(chips, sizes):
     order = np.concatenate([np.arange(0, PAD, 2), np.arange(1, PAD, 2)])
 
     def parts(first, second, sign):
@@ -43,8 +43,9 @@
                 np.concatenate([g_im[:, cut], g_re[:, cut]], 1),
             ]
         )
-    left_focal = np.asarray(left_focal).reshape(2, 2, chips, pieces, rows, PAD)
-    left_focal = left_focal.transpose(0, 3, 1, 2, 4, 5).reshape(2, pieces, P_SIZE * 2 // pieces, PAD)
+    left_focal = np.asarray(left_focal).reshape(2, 2, chips, sum(sizes), PAD)
+    cuts = np.split(left_focal, np.cumsum(sizes)[:-1], axis=3)
+    left_focal = np.concatenate([cut.reshape(2, -1, PAD) for cut in cuts], 1)
     right_focal = np.stack(parts(order, np.arange(PAD), 1.0))
     return [np.asarray(t, dtype=BF16) for t in (left_pupil, right_pupil, left_focal, right_focal)]
 
@@ -86,17 +87,19 @@
 
 
 def kernel(
-    n, pieces, layers, band, points,
-    footprint, fraction, tilt, facet,
-    screens, left_pupil_hbm, right_pupil_hbm, left_focal_hbm, right_focal_hbm,
+    n, sizes, layers, band, points,
+    footprint_hbm, fraction_hbm, tilt_hbm, facet_hbm,
+    screens_hbm, left_pupil_hbm, right_pupil_hbm, left_focal_hbm, right_focal_hbm,
     out,
+    footprint, fraction, tilt, facet, screens,
     lp, rp_in, rp, lf, rf_in, rf,
-    own, snd1, rcv1, snd2, rcv2, fsnd, frcv,
+    own, snd1, rcv1, snd2, rcv2, csnd, crcv,
     modb, mbuf, mk, bk, mask_c, mask_s, both, acc, isnd, ircv, ysnd, yrcv,
-    load_sem, s1, r1, s2, r2, s3, r3, s4, r4, s5, r5,
+    small_sem, load_sem, s1, r1, s2, r2, s3, r3, s4, r4, s5, r5,
 ):
     m = n // 2
-    rows = PAD // n // pieces
+    pieces = len(sizes)
+    offsets = [sum(sizes[:i]) for i in range(pieces)]
     part_rows = HALF // 2
     me = lax.axis_index("mod")
     core = lax.rem(me, 2)
@@ -104,6 +107,17 @@
     other = 1 - core
     partner = chip * 2 + other
 
+    small = [
+        pltpu.make_async_copy(src, dst, small_sem.at[i])
+        for i, (src, dst) in enumerate(
+            (
+                (footprint_hbm, footprint), (fraction_hbm, fraction), (screens_hbm, screens),
+                (tilt_hbm, tilt), (facet_hbm, facet),
+            )
+        )
+    ]
+    for load in small:
+        load.start()
     loads = [
         pltpu.make_async_copy(src, dst, load_sem.at[i])
         for i, (src, dst) in enumerate(
@@ -125,6 +139,8 @@
             device_id={"mod": target}, device_id_type=MESH,
         )
 
+    for load in small:
+        load.wait()
     split = []
     for layer in range(layers):
         frac = fraction[0, 1, layer].astype(F32) / 16.0
@@ -215,22 +231,22 @@
         for k in range(1, m):
             second[q][k - 1].wait()
             code = code + rcv2[k - 1, q].astype(jnp.int32)
-        along_y = 2 * (iota((part_rows, 1), 0) + core * HALF + q * part_rows) - P_SIZE + 1
-        along_x = 2 * iota((1, WIDE), 1) - P_SIZE + 1
-        radius = along_y * along_y + along_x * along_x
-        edge = P_SIZE * 28 // 100 * (P_SIZE * 28 // 100)
-        inside = (radius <= P_SIZE * P_SIZE) & (radius >= edge)
-        cos_part, sin_part = code_parts(code)
-        fsnd[q, 0] = jnp.where(inside, cos_part, 0.0).astype(BF16)
-        fsnd[q, 1] = jnp.where(inside, sin_part, 0.0).astype(BF16)
-        copy = send(fsnd.at[q], frcv.at[q], s3.at[q], r3.at[q], partner)
+        own[q] = code
+        csnd[q] = wrapped(code)
+        copy = send(csnd.at[q], crcv.at[q], s3.at[q], r3.at[q], partner)
         copy.start()
         third.append(copy)
 
-    def pupil_stage(field, which):
+    def pupil_stage(codes, which):
         for q in range(2):
-            wide_re = field[q, 0].astype(F32)
-            wide_im = field[q, 1].astype(F32)
+            along_y = 2 * (iota((part_rows, 1), 0) + which * HALF + q * part_rows) - P_SIZE + 1
+            along_x = 2 * iota((1, WIDE), 1) - P_SIZE + 1
+            radius = along_y * along_y + along_x * along_x
+            edge = P_SIZE * 28 // 100 * (P_SIZE * 28 // 100)
+            inside = (radius <= P_SIZE * P_SIZE) & (radius >= edge)
+            cos_part, sin_part = code_parts(codes[q].astype(jnp.int32))
+            wide_re = jnp.where(inside, cos_part, 0.0).astype(BF16).astype(F32)
+            wide_im = jnp.where(inside, sin_part, 0.0).astype(BF16).astype(F32)
             for p in range(points):
                 row_ids = iota((part_rows, 1), 0) + which * HALF + q * part_rows
                 row_steps = tilt[p, 0].astype(F32) * row_ids.astype(F32)
@@ -249,10 +265,10 @@
             mbuf[pl.ds(start, HALF), p * PAD : (p + 1) * PAD] = wide[cut, :PAD]
             mbuf[pl.ds(start + P_SIZE, HALF), p * PAD : (p + 1) * PAD] = wide[cut, PAD:]
 
-    pupil_stage(fsnd, core)
+    pupil_stage(own, core)
     for copy in third:
         copy.wait()
-    pupil_stage(frcv, other)
+    pupil_stage(crcv, other)
 
     for parity in range(2):
         cut = slice(parity * P_SIZE, (parity + 1) * P_SIZE)
@@ -266,8 +282,11 @@
             mk[parity, P_SIZE:, lanes] = (focal_re * ms + focal_im * mc).astype(BF16)
 
     def focal_stage(piece):
-        even = dot(lf[0, piece], mk[0])
-        odd = dot(lf[1, piece], mk[1])
+        rows = sizes[piece]
+        cut = slice(2 * m * offsets[piece], 2 * m * (offsets[piece] + rows))
+        even = dot(lf[0, cut, :], mk[0])
+        odd = dot(lf[1, cut, :], mk[1])
+        first_row = 2 * points * offsets[piece]
         for sign in range(2):
             value = ((even + odd) if sign == 0 else (even - odd)).astype(BF16)
             for part in range(2):
@@ -275,28 +294,34 @@
                     block = j + sign * m
                     base = (part * m + j) * rows
                     for p in range(points):
-                        spot = ((block % 2) * points + p) * rows
-                        bk[block // 2, piece, spot : spot + rows, part * PAD : (part + 1) * PAD] = value[
+                        spot = first_row + ((block % 2) * points + p) * rows
+                        bk[block // 2, spot : spot + rows, part * PAD : (part + 1) * PAD] = value[
                             base : base + rows, p * PAD : (p + 1) * PAD
                         ]
 
+    def cut_of(piece):
+        return slice(offsets[piece], offsets[piece] + sizes[piece])
+
     waiting = []
 
     def drain():
         while waiting:
-            k, piece, inner = waiting.pop()
+            k, cut, inner = waiting.pop(0)
             inner.wait()
-            ysnd[k - 1, piece] = (acc[k, piece] + ircv[k, piece].astype(F32)).astype(BF16)
+            ysnd[k - 1, cut] = (acc[k, cut] + ircv[k, cut].astype(F32)).astype(BF16)
+            spot = len(pending)
             outer = send(
-                ysnd.at[k - 1, piece], yrcv.at[k - 1, piece], s5.at[k - 1, piece], r5.at[k - 1, piece],
-                lax.rem(me + 2 * k, n),
+                ysnd.at[k - 1, cut], yrcv.at[k - 1, cut], s5.at[spot], r5.at[spot], lax.rem(me + 2 * k, n)
             )
             outer.start()
             pending.append(outer)
 
     def image_stage(k, piece):
+        rows = sizes[piece]
+        cut = cut_of(piece)
         target = lax.rem(chip + k, m)
-        image = dot(bk[target, piece], rf[...])
+        first_row = 2 * points * offsets[piece]
+        image = dot(bk[target, first_row : first_row + 2 * points * rows, :], rf[...])
         power = image[:, :PAD] * image[:, :PAD] + image[:, PAD:] * image[:, PAD:]
         for half in range(2):
             total = None
@@ -304,61 +329,69 @@
                 spot = (half * points + p) * rows
                 term = power[spot : spot + rows]
                 total = term if total is None else total + term
-            both[half] = total
-        isnd[k, piece] = both[other].astype(BF16)
-        acc[k, piece] = both[core]
-        inner = send(isnd.at[k, piece], ircv.at[k, piece], s4.at[k, piece], r4.at[k, piece], partner)
+            both[half, cut] = total
+        isnd[k, cut] = both[other, cut].astype(BF16)
+        acc[k, cut] = both[core, cut]
+        inner = send(isnd.at[k, cut], ircv.at[k, cut], s4.at[k, piece], r4.at[k, piece], partner)
         inner.start()
         return inner
 
     pending = []
     for piece in range(pieces):
         focal_stage(piece)
-        drain()
         for k in range(1, m):
             inner = image_stage(k, piece)
             drain()
-            waiting.append((k, piece, inner))
+            waiting.append((k, cut_of(piece), inner))
     last = []
     for piece in range(pieces):
         last.append(image_stage(0, piece))
         drain()
+    for inner in last:
+        inner.wait()
     for outer in pending:
         outer.wait()
-    for piece in range(pieces):
-        last[piece].wait()
-        total = acc[0, piece] + ircv[0, piece].astype(F32)
-        for k in range(1, m):
-            total = total + yrcv[k - 1, piece].astype(F32)
-        out[0, piece * rows : (piece + 1) * rows] = total * (4.0 / (points * n))
+    total = acc[0] + ircv[0].astype(F32)
+    for k in range(1, m):
+        total = total + yrcv[k - 1].astype(F32)
+    out[0] = total
 
 
 def solution(mesh):
     n = mesh.shape["mod"]
     m = n // 2
     whole_rows = PAD // n
-    pieces = 2 if whole_rows % 32 == 0 else 1
-    rows = whole_rows // pieces
-    consts = tables(m, pieces, rows)
+    units = whole_rows // 16
+    if whole_rows % 16 == 0 and units >= 6:
+        third = units // 3
+        sizes = [16 * (units - 2 * third), 16 * third, 16 * third]
+    else:
+        sizes = [whole_rows]
+    pieces = len(sizes)
+    consts = tables(m, sizes)
     part_rows = HALF // 2
 
     def shards(screens, footprint, fraction, tilt_steps, facet_shift):
         layers, band, width = screens.shape
         points = tilt_steps.shape[0]
-        smem = pl.BlockSpec(memory_space=pltpu.SMEM)
         vmem = pl.BlockSpec(memory_space=pltpu.VMEM)
-        anywhere = pl.BlockSpec(memory_space=pl.ANY)
+        hbm = pl.BlockSpec(memory_space=pltpu.HBM)
         dma = pltpu.SemaphoreType.DMA
-        return pl.pallas_call(
-            functools.partial(kernel, n, pieces, layers, band, points),
+        detector = pl.pallas_call(
+            functools.partial(kernel, n, sizes, layers, band, points),
             out_shape=jax.ShapeDtypeStruct((1, whole_rows, PAD), F32),
-            in_specs=[smem] * 4 + [vmem] + [anywhere] * 4,
+            in_specs=[hbm] * 9,
             out_specs=vmem,
             scratch_shapes=[
+                pltpu.SMEM((1, 2, layers), jnp.int32),
+                pltpu.SMEM((1, 2, layers), jnp.int32),
+                pltpu.SMEM((points, 2), jnp.int32),
+                pltpu.SMEM(facet_shift.shape[::-1], jnp.int32),
+                pltpu.VMEM((layers, band, width), F32),
                 pltpu.VMEM((2, PAD, PAD), BF16),
                 pltpu.VMEM((2, WIDE, PAD), BF16),
                 pltpu.VMEM((2 * WIDE, 2 * PAD), BF16),
-                pltpu.VMEM((2, pieces, 2 * P_SIZE // pieces, PAD), BF16),
+                pltpu.VMEM((2, 2 * P_SIZE, PAD), BF16),
                 pltpu.VMEM((2, PAD, PAD), BF16),
                 pltpu.VMEM((2 * PAD, 2 * PAD), BF16),
                 pltpu.VMEM((2, part_rows, WIDE), jnp.int32),
@@ -366,31 +399,33 @@
                 pltpu.VMEM((2, part_rows, WIDE), jnp.int16),
                 pltpu.VMEM((2, part_rows, WIDE), jnp.int16),
                 pltpu.VMEM((m - 1, 2, part_rows, WIDE), jnp.int16),
-                pltpu.VMEM((2, 2, part_rows, WIDE), BF16),
-                pltpu.VMEM((2, 2, part_rows, WIDE), BF16),
+                pltpu.VMEM((2, part_rows, WIDE), jnp.int16),
+                pltpu.VMEM((2, part_rows, WIDE), jnp.int16),
                 pltpu.VMEM((points * HALF, 2 * WIDE), BF16),
                 pltpu.VMEM((PAD, points * PAD), BF16),
                 pltpu.VMEM((2, PAD, points * PAD), BF16),
-                pltpu.VMEM((m, pieces, 2 * points * rows, 2 * PAD), BF16),
+                pltpu.VMEM((m, 2 * points * whole_rows, 2 * PAD), BF16),
                 pltpu.VMEM((2, P_SIZE, PAD), F32),
                 pltpu.VMEM((2, P_SIZE, PAD), F32),
-                pltpu.VMEM((2, rows, PAD), F32),
-                pltpu.VMEM((m, pieces, rows, PAD), F32),
-                pltpu.VMEM((m, pieces, rows, PAD), BF16),
-                pltpu.VMEM((m, pieces, rows, PAD), BF16),
-                pltpu.VMEM((m - 1, pieces, rows, PAD), BF16),
-                pltpu.VMEM((m - 1, pieces, rows, PAD), BF16),
+                pltpu.VMEM((2, whole_rows, PAD), F32),
+                pltpu.VMEM((m, whole_rows, PAD), F32),
+                pltpu.VMEM((m, whole_rows, PAD), BF16),
+                pltpu.VMEM((m, whole_rows, PAD), BF16),
+                pltpu.VMEM((m - 1, whole_rows, PAD), BF16),
+                pltpu.VMEM((m - 1, whole_rows, PAD), BF16),
+                dma((5,)),
                 dma((4,)),
                 dma((2,)), dma((2,)),
                 dma((m - 1, 2)), dma((m - 1, 2)),
                 dma((2,)), dma((2,)),
                 dma((m, pieces)), dma((m, pieces)),
-                dma((m - 1, pieces)), dma((m - 1, pieces)),
+                dma(((m - 1) * pieces,)), dma(((m - 1) * pieces,)),
             ],
             compiler_params=pltpu.CompilerParams(
                 collective_id=0, has_side_effects=True, vmem_limit_bytes=60 * 1024 * 1024
             ),
         )(footprint.swapaxes(1, 2), fraction.swapaxes(1, 2), tilt_steps, facet_shift.T, screens, *[jnp.asarray(t) for t in consts])
+        return detector * (4.0 / (points * n))
 
     placed = (
         P("group", "mod", None),

time: 31.3 us -> 30.8 us (0.984)
  other arithmetic: 0 us -> 1.78 us
  local copies, waits for them, and re-layouts: 1.78 us -> 0 us
  Pallas kernels: 29.3 us -> 28.8 us
    mul x0 -> x1, other arithmetic: none -> 1.78 us  [shards(): return detector * (4.0 / (points * n))]
    unnamed x1 -> x0, local copies, waits for them, and re-layouts: 1.78 us -> none
    pallas_call x1, Pallas kernels: 29.3 us -> 28.8 us  [shards(): pl.pallas_call(functools.partial(kernel, n, sizes, layers, band, points),...]
where the time goes in v2:
time: 30.8 us; the launch traced here: 30.6 us
  Pallas kernels  28.8 us (94%)
  other arithmetic  1.78 us (6%)
    pallas_call x1, Pallas kernels, shards(): pl.pallas_call(functools.partial(kernel, n, sizes, layers, band, points),...  28.8 us
    mul x1, other arithmetic, shards(): return detector * (4.0 / (points * n))  1.78 us

profile of v2, /device:TPU:0, one launch (start us, length us, event | category | flops | bytes accessed | tf_op | source)
XLA Modules:
  0.0 30.6 jit_solution(6754462426554348642)
XLA Ops:
  0.0 28.8 %shard_map.91 = f32[1,160,640]{2,1,0:T(8,128)} custom-call(s32[1,2,4]{2,1,0:T(2,128)} %bitcast.3, s32[1,2,4]{2,1,0:T(2,128)} %bitcast.4, s32[2,2]{1,0:T(2,128)} %tilt_hbm.1, s32[2,4]{1,0:T(2,128)} %bitcast.5, f32[4,128,512]{2,1,0:T(8,128)} %screens_hbm.1, bf16[2,640,640]{2,1,0:T(8,128)(2,1)} %constant.10.clone.left_pupil_hbm, ...), custom_call_target="tpu_custom_call" | custom-call | tf_op jit(solution)/shard_map/pallas_call | solution.py:380
  28.8 1.8 %broadcast_multiply_fusion = f32[1,160,640]{2,1,0:T(8,128)} fusion(f32[1,160,640]{2,1,0:T(8,128)} %shard_map.91), kind=kLoop, calls=%fused_computation | loop fusion | flops 102400 | bytes 819200 | tf_op jit(solution)/shard_map/mul | solution.py:428

commit v3 on v2

--- a/solution.py
+++ b/solution.py
@@ -422,7 +422,7 @@
                 dma(((m - 1) * pieces,)), dma(((m - 1) * pieces,)),
             ],
             compiler_params=pltpu.CompilerParams(
-                collective_id=0, has_side_effects=True, vmem_limit_bytes=60 * 1024 * 1024
+                collective_id=0, has_side_effects=True, vmem_limit_bytes=53 * 1024 * 1024
             ),
         )(footprint.swapaxes(1, 2), fraction.swapaxes(1, 2), tilt_steps, facet_shift.T, screens, *[jnp.asarray(t) for t in consts])
         return detector * (4.0 / (points * n))

time: 30.8 us -> 31.8 us (1.032)
  local copies, waits for them, and re-layouts: 0 us -> 2.71 us
  other arithmetic: 1.78 us -> 0.78 us
  Pallas kernels: 28.8 us -> 28.1 us
    unnamed x0 -> x8, local copies, waits for them, and re-layouts: none -> 2.71 us
    mul x1, other arithmetic: 1.78 us -> 0.78 us  [shards(): return detector * (4.0 / (points * n))]
    pallas_call x1, Pallas kernels: 28.8 us -> 28.1 us  [shards(): pl.pallas_call(functools.partial(kernel, n, sizes, layers, band, points),...]
where the time goes in v3:
time: 31.8 us; the launch traced here: 31.6 us
  Pallas kernels  28.1 us (88%)
  local copies, waits for them, and re-layouts  2.71 us (9%)
  other arithmetic  0.78 us (2%)
    pallas_call x1, Pallas kernels, shards(): pl.pallas_call(functools.partial(kernel, n, sizes, layers, band, points),...  28.1 us
    unnamed x8, local copies, waits for them, and re-layouts  2.71 us
    mul x1, other arithmetic, shards(): return detector * (4.0 / (points * n))  0.78 us

profile of v3, /device:TPU:0, one launch (start us, length us, event | category | flops | bytes accessed | tf_op | source)
XLA Modules:
  0.0 31.6 jit_solution(17480577105549345734)
XLA Ops:
  0.0 0.0 copy-start
  0.0 0.7 %copy-done = s32[1,4,2]{1,2,0:T(2,128)S(1)} copy-done((s32[1,4,2]{1,2,0:T(2,128)S(1)}, s32[1,4,2]{1,2,0:T(2,128)}, u32[]{:S(2)}) %copy-start) | copy-done | bytes 56
  0.7 0.0 copy-start.1
  0.7 0.7 %copy-done.1 = s32[1,4,2]{1,2,0:T(2,128)S(1)} copy-done((s32[1,4,2]{1,2,0:T(2,128)S(1)}, s32[1,4,2]{1,2,0:T(2,128)}, u32[]{:S(2)}) %copy-start.1) | copy-done | bytes 56
  1.4 0.0 copy-start.2
  1.4 0.7 %copy-done.2 = s32[2,2]{1,0:T(2,128)S(1)} copy-done((s32[2,2]{1,0:T(2,128)S(1)}, s32[2,2]{1,0:T(2,128)}, u32[]{:S(2)}) %copy-start.2) | copy-done | bytes 40
  2.0 0.0 copy-start.3
  2.0 0.7 %copy-done.3 = s32[4,2]{0,1:T(2,128)S(1)} copy-done((s32[4,2]{0,1:T(2,128)S(1)}, s32[4,2]{0,1:T(2,128)}, u32[]{:S(2)}) %copy-start.3) | copy-done | bytes 56
  2.7 28.1 %shard_map.91 = f32[1,160,640]{2,1,0:T(8,128)S(1)} custom-call(s32[1,2,4]{2,1,0:T(2,128)S(1)} %bitcast.3, s32[1,2,4]{2,1,0:T(2,128)S(1)} %bitcast.4, s32[2,2]{1,0:T(2,128)S(1)} %copy-done.2, s32[2,4]{1,0:T(2,128)S(1)} %bitcast.5, f32[4,128,512]{2,1,0:T(8,128)} %screens_hbm.1, bf16[2,640,640]{2,1,0:T(8,128)(2,1)} %constant.10.clone.left_pupil_hbm, ...), custom_call_target="tpu_custom_call" | custom-call | tf_op jit(solution)/shard_map/pallas_call | solution.py:380
  30.8 0.8 %broadcast_multiply_fusion = f32[1,160,640]{2,1,0:T(8,128)} fusion(f32[1,160,640]{2,1,0:T(8,128)S(1)} %shard_map.91), kind=kLoop, calls=%fused_computation | loop fusion | flops 102400 | bytes 819200 | tf_op jit(solution)/shard_map/mul | solution.py:428
Async XLA Ops:
  0.0 0.7 %copy-start = (s32[1,4,2]{1,2,0:T(2,128)S(1)}, s32[1,4,2]{1,2,0:T(2,128)}, u32[]{:S(2)}) copy-start(s32[1,4,2]{1,2,0:T(2,128)} %param.10) | copy-start | bytes 100
  0.7 0.7 %copy-start.1 = (s32[1,4,2]{1,2,0:T(2,128)S(1)}, s32[1,4,2]{1,2,0:T(2,128)}, u32[]{:S(2)}) copy-start(s32[1,4,2]{1,2,0:T(2,128)} %param.11) | copy-start | bytes 100
  1.4 0.7 %copy-start.2 = (s32[2,2]{1,0:T(2,128)S(1)}, s32[2,2]{1,0:T(2,128)}, u32[]{:S(2)}) copy-start(s32[2,2]{1,0:T(2,128)} %tilt_hbm.1) | copy-start | bytes 52
  2.0 0.7 %copy-start.3 = (s32[4,2]{0,1:T(2,128)S(1)}, s32[4,2]{0,1:T(2,128)}, u32[]{:S(2)}) copy-start(s32[4,2]{0,1:T(2,128)} %param.13) | copy-start | bytes 100
